TPU v7x, 256 devices: a whole 4x4x8 slice. The times are simulated.
256 devices in a mesh: dp: 8 (over y, core), expert: 32 (over z, x).
Axes of the slice: x: 4, y: 4, z: 8, core: 2. Of those that a mesh axis runs over, the one named last changes fastest.
Arguments:
- tokens: bfloat16 [32768, 2048], P(('dp', 'expert')), may hold values from -6 to 6
- expert_ids: int32 [32768, 8], P(('dp', 'expert')), may hold values from 0 to 31, all different within a row
- gate_vals: float32 [32768, 8], P(('dp', 'expert')), may hold values from 0.05 to 0.5
- replica_plan: int32 [32], replicated, may hold values from 0 to 1, as said below
- expert_weights: bfloat16 [32, 3, 2048, 768], P('expert'), may hold values from -0.125 to 0.125
- cotangent: bfloat16 [32768, 2048], P(('dp', 'expert')), may hold values from -6 to 6
Outputs:
- output: bfloat16 [32768, 2048], P(('dp', 'expert'))
- gate_grads: float32 [32768, 8], P(('dp', 'expert'))
- input_grad: bfloat16 [32768, 2048], P(('dp', 'expert'))
- weight_grads: bfloat16 [32, 3, 2048, 768], P('expert', None, 'dp')
Inputs may be any that keep to these rules, and one draw needn't show every extreme that they name: `replica_plan`: of experts x and x + 16 exactly one is marked.
All inputs are finite; a program needn't handle non-finite values.
Results may differ from a plain program's by a relative error of at most 0.017.
Values may be sent and summed in bfloat16 or wider, within the bound.
A program may use at most 128 MiB of HBM per device.

v0:
```python
import jax
import jax.numpy as jnp
from jax import lax
from jax.sharding import PartitionSpec as P


def forward(rows, weights):
    gate_part = jnp.dot(rows, weights[0], preferred_element_type=jnp.float32)
    up_part = jnp.dot(rows, weights[1], preferred_element_type=jnp.float32)
    sigma = jax.nn.sigmoid(gate_part)
    hidden = (gate_part * sigma * up_part).astype(jnp.bfloat16)
    result = lax.dot_general(
        hidden, weights[2], (((1,), (1,)), ((), ())), preferred_element_type=jnp.float32
    ).astype(jnp.bfloat16)
    return (hidden, result, gate_part, up_part)


def backward(cotan, gate_part, up_part, weights):
    hgrad = jnp.dot(cotan, weights[2], preferred_element_type=jnp.float32)
    sigma = jax.nn.sigmoid(gate_part)
    d_gate = (hgrad * up_part * sigma * (1.0 + gate_part * (1.0 - sigma))).astype(jnp.bfloat16)
    d_up = (hgrad * (gate_part * sigma)).astype(jnp.bfloat16)
    row_grad = (
        lax.dot_general(
            d_gate, weights[0], (((1,), (1,)), ((), ())), preferred_element_type=jnp.float32
        )
        + lax.dot_general(
            d_up, weights[1], (((1,), (1,)), ((), ())), preferred_element_type=jnp.float32
        )
    ).astype(jnp.bfloat16)
    return (d_gate, d_up, row_grad)


def blank_forward(count, hidden_units, width):
    return (
        jnp.zeros((count, hidden_units), jnp.bfloat16),
        jnp.zeros((count, width), jnp.bfloat16),
        jnp.zeros((count, hidden_units), jnp.float32),
        jnp.zeros((count, hidden_units), jnp.float32),
    )


def blank_backward(count, hidden_units, width):
    return (
        jnp.zeros((count, hidden_units), jnp.bfloat16),
        jnp.zeros((count, hidden_units), jnp.bfloat16),
        jnp.zeros((count, width), jnp.bfloat16),
    )


def per_device(tokens, expert_ids, gate_vals, replica_plan, expert_weights, cotangent):
    tok_rows, width = tokens.shape
    topk = expert_ids.shape[1]
    experts = replica_plan.shape[0]
    hidden_units = expert_weights.shape[3]
    cap = tok_rows * topk * 5 // (16 * experts)
    slots = 2 * cap
    total = experts * slots
    here = lax.axis_index("expert")
    weights = expert_weights[0]
    flat = expert_ids.reshape(-1)
    labels = jnp.arange(experts, dtype=jnp.int32)
    onehot = (flat[:, None] == labels[None, :]).astype(jnp.int32)
    rank = jnp.sum((jnp.cumsum(onehot, axis=0) - onehot) * onehot, axis=1)
    marked = jnp.sum(onehot * replica_plan[None, :], axis=1)
    keep = (rank < cap) | (marked == 1) & (rank < slots)
    target = jnp.where(keep, flat * slots + rank, total)
    places = jnp.arange(total, dtype=jnp.int32)
    match = target[:, None] == places[None, :]
    spread = jnp.sum(match.astype(jnp.bfloat16).reshape(tok_rows, topk, total), axis=1)
    slot_gate = jnp.sum(jnp.where(match, gate_vals.reshape(-1)[:, None], 0.0), axis=0)
    own_flag = jnp.sum(jnp.where(labels == here, replica_plan, 0))
    contract_rows = (((0,), (0,)), ((), ()))
    send = lax.dot_general(
        spread, tokens, contract_rows, preferred_element_type=jnp.float32
    ).astype(jnp.bfloat16)
    dy_buffer = lax.dot_general(
        spread, cotangent, contract_rows, preferred_element_type=jnp.float32
    )
    dy_send = (slot_gate[:, None] * dy_buffer).astype(jnp.bfloat16)
    arrived = lax.all_to_all(
        send.reshape(experts, slots, width), "expert", split_axis=0, concat_axis=0, tiled=True
    )
    dy_arrived = lax.all_to_all(
        dy_send.reshape(experts, slots, width), "expert", split_axis=0, concat_axis=0, tiled=True
    )
    first = arrived[:, :cap].reshape(-1, width)
    second = arrived[:, cap:].reshape(-1, width)
    count = first.shape[0]
    hid_one, out_one, gate_one, up_one = forward(first, weights)
    hid_two, out_two, gate_two, up_two = lax.cond(
        own_flag == 1,
        lambda: forward(second, weights),
        lambda: blank_forward(count, hidden_units, width),
    )
    out_buffer = jnp.concatenate(
        [out_one.reshape(experts, cap, width), out_two.reshape(experts, cap, width)], axis=1
    )
    returned = lax.all_to_all(
        out_buffer, "expert", split_axis=0, concat_axis=0, tiled=True
    ).reshape(total, width)
    valid = (target < total)[:, None]
    index = jnp.minimum(target, total - 1)
    pair_out = jnp.where(valid, jnp.take(returned, index, axis=0).astype(jnp.float32), 0.0).reshape(
        tok_rows, topk, width
    )
    output = jnp.sum(gate_vals[:, :, None] * pair_out, axis=1).astype(jnp.bfloat16)
    gate_grads = jnp.sum(cotangent.astype(jnp.float32)[:, None, :] * pair_out, axis=2)
    dy_one = dy_arrived[:, :cap].reshape(-1, width)
    dy_two = dy_arrived[:, cap:].reshape(-1, width)
    dgate_one, dup_one, rgrad_one = backward(dy_one, gate_one, up_one, weights)
    dgate_two, dup_two, rgrad_two = lax.cond(
        own_flag == 1,
        lambda: backward(dy_two, gate_two, up_two, weights),
        lambda: blank_backward(count, hidden_units, width),
    )
    grad_buffer = jnp.concatenate(
        [rgrad_one.reshape(experts, cap, width), rgrad_two.reshape(experts, cap, width)], axis=1
    )
    grad_back = lax.all_to_all(
        grad_buffer, "expert", split_axis=0, concat_axis=0, tiled=True
    ).reshape(total, width)
    pair_grad = jnp.where(
        valid, jnp.take(grad_back, index, axis=0).astype(jnp.float32), 0.0
    ).reshape(tok_rows, topk, width)
    input_grad = jnp.sum(pair_grad, axis=1).astype(jnp.bfloat16)
    left_rows = jnp.concatenate([first, second], axis=0)
    cot_rows = jnp.concatenate([dy_one, dy_two], axis=0)
    hid_rows = jnp.concatenate([hid_one, hid_two], axis=0)
    pre_grads = jnp.concatenate(
        [
            jnp.concatenate([dgate_one, dgate_two], axis=0),
            jnp.concatenate([dup_one, dup_two], axis=0),
        ],
        axis=1,
    )
    per_dev = width // lax.axis_size("dp")
    upper = lax.dot_general(left_rows, pre_grads, contract_rows, preferred_element_type=jnp.float32)
    lower = lax.dot_general(cot_rows, hid_rows, contract_rows, preferred_element_type=jnp.float32)
    shard = lax.psum_scatter(
        jnp.concatenate([upper, lower], axis=1).astype(jnp.bfloat16),
        "dp",
        scatter_dimension=0,
        tiled=True,
    ).astype(jnp.float32)
    weight_grads = (
        shard.reshape(per_dev, 3, hidden_units).transpose(1, 0, 2)[None].astype(jnp.bfloat16)
    )
    return (output, gate_grads, input_grad, weight_grads)


def solution(mesh):
    in_specs = (
        P(("dp", "expert"), None),
        P(("dp", "expert"), None),
        P(("dp", "expert"), None),
        P(),
        P("expert", None, None, None),
        P(("dp", "expert"), None),
    )
    out_specs = (
        P(("dp", "expert"), None),
        P(("dp", "expert"), None),
        P(("dp", "expert"), None),
        P("expert", None, "dp", None),
    )
    return jax.shard_map(
        per_device, mesh=mesh, in_specs=in_specs, out_specs=out_specs, check_vma=False
    )
```

profile of v0, /device:TPU:16, one launch (start us, length us, event | category | flops | bytes accessed | tf_op | source)
XLA Modules:
  0.0 479.8 jit_solution(11416483358236920159)
XLA Ops:
  9.0 9.0 %reduce-window.6 = s32[32,8,128]{2,1,0:T(8,128)S(1)} reduce-window(s32[32,8,128]{2,1,0:T(8,128)S(1)} %fusion.78, s32[]{:T(128)} %constant.9.clone.1), window={size=1x1x128 pad=0_0x0_0x127_0}, to_apply=%region_0.0 | reduce-window | flops 4161536 | bytes 262148 | tf_op jit(solution)/shard_map/reduce-window
  25.8 11.4 %all-to-all-start.2 = ((bf16[32,20,2048]{2,1,0:T(8,128)(2,1)}), bf16[32,20,2048]{2,1,0:T(8,128)(2,1)}, u32[]{:S(2)}, u32[]{:S(2)}) async-start(bf16[32,20,2048]{2,1,0:T(8,128)(2,1)} %reshape.141), calls=%async_computation.2 | async-start | bytes 6291456 | tf_op jit(solution)/shard_map/all_to_all | solution.py:84
  40.5 69.0 %all-to-all-done.2 = bf16[32,20,2048]{2,1,0:T(8,128)(2,1)} async-done(((bf16[32,20,2048]{2,1,0:T(8,128)(2,1)}), bf16[32,20,2048]{2,1,0:T(8,128)(2,1)}, u32[]{:S(2)}, u32[]{:S(2)}) %all-to-all-start.2) | async-done | bytes 2621472 | tf_op jit(solution)/shard_map/all_to_all | solution.py:84
  109.5 6.4 %all-to-all-start = ((bf16[32,20,2048]{2,1,0:T(8,128)(2,1)}), bf16[32,20,2048]{2,1,0:T(8,128)(2,1)}, u32[]{:S(2)}, u32[]{:S(2)}) async-start(bf16[32,20,2048]{2,1,0:T(8,128)(2,1)} %reshape.135), calls=%async_computation | async-start | bytes 6291456 | tf_op jit(solution)/shard_map/all_to_all | solution.py:81
  117.3 4.6 fusion.84
  125.5 62.3 %all-to-all-done = bf16[32,20,2048]{2,1,0:T(8,128)(2,1)} async-done(((bf16[32,20,2048]{2,1,0:T(8,128)(2,1)}), bf16[32,20,2048]{2,1,0:T(8,128)(2,1)}, u32[]{:S(2)}, u32[]{:S(2)}) %all-to-all-start) | async-done | bytes 2621472 | tf_op jit(solution)/shard_map/all_to_all | solution.py:81
  187.9 5.5 %fusion.83 = (bf16[32,10,2048]{2,1,0:T(8,128)(2,1)}, bf16[32,10,2048]{2,1,0:T(8,128)(2,1)}) fusion(bf16[32,20,2048]{2,1,0:T(8,128)(2,1)} %all-to-all-done), kind=kLoop, calls=%fused_computation.109 | loop fusion | bytes 5242880 | tf_op jit(solution)/shard_map/slice | solution.py:87
  201.8 4.5 fusion.39
  206.3 4.2 fusion.29
  215.8 4.4 multiply_convert_fusion.6
  220.3 5.9 %convolution_convert_fusion.1 = bf16[2048,768]{0,1:T(8,128)(2,1)S(1)} fusion(bf16[320,2048]{1,0:T(8,128)(2,1)S(1)} %copy-done.3, bf16[320,2048]{1,0:T(8,128)(2,1)S(1)} %copy-done.8, bf16[320,768]{1,0:T(8,128)(2,1)} %get-tuple-element.38, bf16[320,768]{1,0:T(8,128)(2,1)S(1)} %get-tuple-element.62), kind=kOutput, calls=%fused_computation.37 | convolution fusion | flops 2022047744 | bytes 6750208 | tf_op jit(solution)/shard_map/dot_general | solution.py:139
  226.2 11.6 %convolution_convert_fusion = bf16[2048,1536]{0,1:T(8,128)(2,1)S(1)} fusion(bf16[320,2048]{1,0:T(8,128)(2,1)S(1)} %copy-done.5, bf16[320,2048]{1,0:T(8,128)(2,1)S(1)} %copy-done.6, bf16[320,768]{1,0:T(8,128)(2,1)S(1)} %get-tuple-element.37, bf16[320,768]{1,0:T(8,128)(2,1)S(1)} %get-tuple-element.64, bf16[320,768]{1,0:T(8,128)(2,1)S(1)} %get-tuple-element.36, ...), kind=kOutput, calls=%fused_computation.34 | convolution fusion | flops 4042784768 | bytes 10878976 | tf_op jit(solution)/shard_map/dot_general | solution.py:138
  237.8 11.4 %pad_maximum_fusion = bf16[2048,2304]{0,1:T(8,128)(2,1)} fusion(bf16[2048,768]{0,1:T(8,128)(2,1)S(1)} %convolution_convert_fusion.1, bf16[2048,1536]{0,1:T(8,128)(2,1)S(1)} %convolution_convert_fusion), kind=kLoop, calls=%fused_computation.27 | loop fusion | flops 18874368 | bytes 18874368 | tf_op jit(solution)/shard_map/concatenate | solution.py:141
  253.4 4.2 fusion.50
  261.1 4.9 %pad_maximum_fusion.2 = bf16[32,20,2048]{2,1,0:T(8,128)(2,1)} fusion(bf16[32,10,2048]{2,1,0:T(8,128)(2,1)} %get-tuple-element.35, bf16[32,10,2048]{2,1,0:T(8,128)(2,1)} %reshape.143), kind=kLoop, calls=%fused_computation.40 | loop fusion | flops 5242880 | bytes 5242880 | tf_op jit(solution)/shard_map/concatenate | solution.py:117
  266.0 29.4 %all-to-all-start.3 = ((bf16[32,20,2048]{2,1,0:T(8,128)(2,1)}), bf16[32,20,2048]{2,1,0:T(8,128)(2,1)}, u32[]{:S(2)}, u32[]{:S(2)}) async-start(bf16[32,20,2048]{2,1,0:T(8,128)(2,1)} %pad_maximum_fusion.2), calls=%async_computation.3 | async-start | bytes 6291456 | tf_op jit(solution)/shard_map/all_to_all | solution.py:120
  295.5 4.2 fusion.53
  303.1 4.2 pad_maximum_fusion.1
  307.3 59.0 %all-to-all-done.3 = bf16[32,20,2048]{2,1,0:T(8,128)(2,1)} async-done(((bf16[32,20,2048]{2,1,0:T(8,128)(2,1)}), bf16[32,20,2048]{2,1,0:T(8,128)(2,1)}, u32[]{:S(2)}, u32[]{:S(2)}) %all-to-all-start.3) | async-done | bytes 2621472 | tf_op jit(solution)/shard_map/all_to_all | solution.py:120
  366.3 6.4 %all-to-all-start.1 = ((bf16[32,20,2048]{2,1,0:T(8,128)(2,1)}), bf16[32,20,2048]{2,1,0:T(8,128)(2,1)}, u32[]{:S(2)}, u32[]{:S(2)}) async-start(bf16[32,20,2048]{2,1,0:T(8,128)(2,1)} %pad_maximum_fusion.1), calls=%async_computation.1 | async-start | bytes 6291456 | tf_op jit(solution)/shard_map/all_to_all | solution.py:99
  377.5 6.0 %gather_fusion.1 = bf16[1024,2048]{1,0:T(8,128)(2,1)} fusion(bf16[640,2048]{1,0:T(8,128)(2,1)S(1)} %reshape.145, s32[1024]{0:T(1024)S(1)} %fusion.79), kind=kCustom, calls=%fused_computation.1.clone | custom fusion | bytes 8392704 | tf_op jit(solution)/shard_map/jit(_take)/gather | solution.py:124
  383.5 60.4 %all-to-all-done.1 = bf16[32,20,2048]{2,1,0:T(8,128)(2,1)} async-done(((bf16[32,20,2048]{2,1,0:T(8,128)(2,1)}), bf16[32,20,2048]{2,1,0:T(8,128)(2,1)}, u32[]{:S(2)}, u32[]{:S(2)}) %all-to-all-start.1) | async-done | bytes 2621472 | tf_op jit(solution)/shard_map/all_to_all | solution.py:99
  447.5 6.0 %gather_fusion = bf16[1024,2048]{1,0:T(8,128)(2,1)} fusion(bf16[640,2048]{1,0:T(8,128)(2,1)S(1)} %reshape.139, s32[1024]{0:T(1024)S(1)} %fusion.79), kind=kCustom, calls=%fused_computation.clone | custom fusion | bytes 8392704 | tf_op jit(solution)/shard_map/jit(_take)/gather | solution.py:104
  457.9 12.4 %bitcast_reduce_fusion = (bf16[128,2048]{1,0:T(8,128)(2,1)}, bf16[128,2048]{1,0:T(8,128)(2,1)}) fusion(bf16[1024,2048]{1,0:T(8,128)(2,1)} %gather_fusion.1, pred[1024]{0:T(1024)(128)(4,1)S(1)} %compare_and_fusion, pred[1024]{0:T(1024)(128)(4,1)S(1)} %get-tuple-element.51, bf16[1024,2048]{1,0:T(8,128)(2,1)} %gather_fusion, f32[128,8]{1,0:T(8,128)S(1)} %copy.23), kind=kLoop, calls=%fused_computation.28 | loop fusion | flops 18350080 | bytes 9443328 | tf_op jit(solution)/shard_map/reduce_sum | solution.py:126
  (86 shorter events, 61.9 us)
Async XLA Ops:
  7.2 30.1 %copy-start = (bf16[128,2048]{1,0:T(8,128)(2,1)S(1)}, bf16[128,2048]{1,0:T(8,128)(2,1)}, u32[]{:S(2)}) copy-start(bf16[128,2048]{1,0:T(8,128)(2,1)} %param.12) | copy-start | bytes 1572868
  25.8 83.7 %all-to-all-start.2 = ((bf16[32,20,2048]{2,1,0:T(8,128)(2,1)}), bf16[32,20,2048]{2,1,0:T(8,128)(2,1)}, u32[]{:S(2)}, u32[]{:S(2)}) async-start(bf16[32,20,2048]{2,1,0:T(8,128)(2,1)} %reshape.141), calls=%async_computation.2 | async-start | bytes 6291456 | tf_op jit(solution)/shard_map/all_to_all | solution.py:84
  40.5 75.5 %copy-start.13 = (s32[32]{0:T(128)S(1)}, s32[32]{0:T(128)}, u32[]{:S(2)}) copy-start(s32[32]{0:T(128)} %param.15) | copy-start | bytes 388
  109.5 78.3 %all-to-all-start = ((bf16[32,20,2048]{2,1,0:T(8,128)(2,1)}), bf16[32,20,2048]{2,1,0:T(8,128)(2,1)}, u32[]{:S(2)}, u32[]{:S(2)}) async-start(bf16[32,20,2048]{2,1,0:T(8,128)(2,1)} %reshape.135), calls=%async_computation | async-start | bytes 6291456 | tf_op jit(solution)/shard_map/all_to_all | solution.py:81
  115.9 354.5 %reduce-scatter.2.cloned.1.call-start = ((), (), s32[]{:S(2)}) async-start(), calls=%async_computation.5 | async-start | bytes 10616832 | tf_op jit(solution)/shard_map/reduce_scatter | solution.py:140
  201.8 4.6 copy-start.7
  206.3 4.2 copy-start.4
  215.8 4.4 copy-start.3
  215.8 4.4 copy-start.8
  220.2 6.0 %copy-start.19 = (bf16[320,768]{1,0:T(8,128)(2,1)}, bf16[320,768]{1,0:T(8,128)(2,1)S(1)}, u32[]{:S(2)}) copy-start(bf16[320,768]{1,0:T(8,128)(2,1)S(1)} %get-tuple-element.62) | copy-start | bytes 1474564
  220.2 6.0 %copy-start.15 = (bf16[320,768]{1,0:T(8,128)(2,1)}, bf16[320,768]{1,0:T(8,128)(2,1)S(1)}, u32[]{:S(2)}) copy-start(bf16[320,768]{1,0:T(8,128)(2,1)S(1)} %get-tuple-element.64) | copy-start | bytes 1474564
  220.2 6.0 %copy-start.17 = (bf16[320,768]{1,0:T(8,128)(2,1)}, bf16[320,768]{1,0:T(8,128)(2,1)S(1)}, u32[]{:S(2)}) copy-start(bf16[320,768]{1,0:T(8,128)(2,1)S(1)} %get-tuple-element.63) | copy-start | bytes 1474564
  220.3 6.0 %copy-start.5 = (bf16[320,2048]{1,0:T(8,128)(2,1)S(1)}, bf16[320,2048]{1,0:T(8,128)(2,1)}, u32[]{:S(2)}) copy-start(bf16[320,2048]{1,0:T(8,128)(2,1)} %reshape.138) | copy-start | bytes 3932164
  220.3 6.0 %copy-start.6 = (bf16[320,2048]{1,0:T(8,128)(2,1)S(1)}, bf16[320,2048]{1,0:T(8,128)(2,1)}, u32[]{:S(2)}) copy-start(bf16[320,2048]{1,0:T(8,128)(2,1)} %reshape.136) | copy-start | bytes 3932164
  249.2 1.0 copy-start.16
  250.3 3.2 copy-start.18
  266.0 29.4 %copy-start.20 = (bf16[320,768]{1,0:T(8,128)(2,1)S(1)}, bf16[320,768]{1,0:T(8,128)(2,1)}, u32[]{:S(2)}) copy-start(bf16[320,768]{1,0:T(8,128)(2,1)} %copy-done.19) | copy-start | bytes 1474564
  266.0 100.3 %all-to-all-start.3 = ((bf16[32,20,2048]{2,1,0:T(8,128)(2,1)}), bf16[32,20,2048]{2,1,0:T(8,128)(2,1)}, u32[]{:S(2)}, u32[]{:S(2)}) async-start(bf16[32,20,2048]{2,1,0:T(8,128)(2,1)} %pad_maximum_fusion.2), calls=%async_computation.3 | async-start | bytes 6291456 | tf_op jit(solution)/shard_map/all_to_all | solution.py:120
  307.3 65.4 %copy-start.2 = (bf16[128,2048]{1,0:T(8,128)(2,1)S(1)}, bf16[128,2048]{1,0:T(8,128)(2,1)}, u32[]{:S(2)}) copy-start(bf16[128,2048]{1,0:T(8,128)(2,1)} %param.17) | copy-start | bytes 1572868
  366.3 77.6 %all-to-all-start.1 = ((bf16[32,20,2048]{2,1,0:T(8,128)(2,1)}), bf16[32,20,2048]{2,1,0:T(8,128)(2,1)}, u32[]{:S(2)}, u32[]{:S(2)}) async-start(bf16[32,20,2048]{2,1,0:T(8,128)(2,1)} %pad_maximum_fusion.1), calls=%async_computation.1 | async-start | bytes 6291456 | tf_op jit(solution)/shard_map/all_to_all | solution.py:99
  457.9 14.8 %copy-start.1 = (bf16[128,2048]{1,0:T(8,128)(2,1)S(1)}, bf16[128,2048]{1,0:T(8,128)(2,1)}, u32[]{:S(2)}) copy-start(bf16[128,2048]{1,0:T(8,128)(2,1)} %param.12) | copy-start | bytes 1572868
Sparse Core Ops, SparseCore 0:
  249.4 77.6 reduce-scatter.1
where the time goes:
time: 489 us; the launch traced here: 480 us
  waiting for transfers between devices  251 us (51%)
  local copies, waits for them, and re-layouts  64.4 us (13%)
  starting transfers between devices  53.7 us (11%)
  other arithmetic  50.2 us (10%)
  matrix products  44.9 us (9%)
  between operations  15.3 us (3%)
    all_to_all x1, waiting for transfers between devices, per_device(): lax.all_to_all(dy_send.reshape(experts, slots, width), 'expert', split_ax...  69 us
    all_to_all x1, waiting for transfers between devices, per_device(): lax.all_to_all(send.reshape(experts, slots, width), 'expert', split_axis=...  62.3 us
    all_to_all x1, waiting for transfers between devices, per_device(): lax.all_to_all(out_buffer, 'expert', split_axis=0, concat_axis=0, tiled=T...  60.4 us
    all_to_all x1, waiting for transfers between devices, per_device(): lax.all_to_all(grad_buffer, 'expert', split_axis=0, concat_axis=0, tiled=...  59 us
    all_to_all x1, starting transfers between devices, per_device(): lax.all_to_all(grad_buffer, 'expert', split_axis=0, concat_axis=0, tiled=...  29.4 us
    reduce_sum x1, other arithmetic, per_device(): input_grad = jnp.sum(pair_grad, axis=1).astype(jnp.bfloat16)  12.4 us
    dot_general x1, matrix products, per_device(): lax.dot_general(left_rows, pre_grads, contract_rows, preferred_element_ty...  11.6 us
    all_to_all x1, starting transfers between devices, per_device(): lax.all_to_all(dy_send.reshape(experts, slots, width), 'expert', split_ax...  11.4 us
  transfers between devices with their start and end apart: 5, of which 4 were waited for; matrix products, arithmetic and copies ran while one was open for 16% of the time, Pallas kernels for 0%

commit v1 on v0

v1 whole, which is shorter than its diff:
```python
import functools

import jax
import jax.numpy as jnp
from jax import lax
from jax.experimental import pallas as pl
from jax.experimental.pallas import tpu as pltpu
from jax.sharding import PartitionSpec as P

COLS = 4
RING = 8
HOPS = 3
FAR = 6
PAIRS = 4
LANES = 128
BF16, F32 = jnp.bfloat16, jnp.float32


def place():
    here = lax.axis_index("expert")
    z, x = here // COLS, here % COLS
    up = ((z + 1) % RING) * COLS + x
    down = ((z + RING - 1) % RING) * COLS + x
    right = [z * COLS + (x + d) % COLS for d in range(COLS)]
    left = [z * COLS + (x + COLS - d) % COLS for d in range(COLS)]
    return z, x, up, down, right, left


def copy_to(src, dst, send_sem, recv_sem, device):
    return pltpu.make_async_remote_copy(
        src_ref=src,
        dst_ref=dst,
        send_sem=send_sem,
        recv_sem=recv_sem,
        device_id={"expert": device},
        device_id_type=pl.DeviceIdType.MESH,
    )


def meet(up, down, right):
    barrier = pltpu.get_barrier_semaphore()
    peers = [up, down] + right[1:]
    for peer in peers:
        pl.semaphore_signal(
            barrier, inc=1, device_id={"expert": peer}, device_id_type=pl.DeviceIdType.MESH
        )
    pl.semaphore_wait(barrier, len(peers))


def dispatch_kernel(
    cap, plan, tok, cot, info, tok_rows, cot_rows, spread,
    tok_ring, cot_ring, info_ring, tok_sel, cot_sel,
    ring_send, ring_recv, row_send, row_recv, own_sem,
):
    z, x, up, down, right, _ = place()
    count, width = tok.shape
    half = count // 2
    slots = 2 * cap
    rows = 2 * slots
    meet(up, down, right)

    own = (tok, cot, info)
    ring = (tok_ring, cot_ring, info_ring)

    def slot(way, d):
        return FAR if d > HOPS else way * HOPS + d - 1

    def hop(q, way, d):
        src = own[q] if d == 1 else ring[q].at[slot(way, d - 1)]
        dst = ring[q].at[slot(way, d)]
        if d > HOPS and q < 2:
            src, dst = src.at[pl.ds(way * half, half)], dst.at[pl.ds(way * half, half)]
        sem = way * (HOPS + 1) + d - 1
        return copy_to(
            src, dst, ring_send.at[q, sem], ring_recv.at[q, sem], down if way else up
        )

    hops = {
        (q, way, d): hop(q, way, d)
        for q in range(3)
        for way in range(2)
        for d in range(1, HOPS + 2)
        if not (q == 2 and way == 1 and d > HOPS)
    }
    for q in (2, 0, 1):
        for way in range(2):
            hops[q, way, 1].start()

    lane = lax.broadcasted_iota(jnp.int32, (count, count), 1)
    before = lax.broadcasted_iota(jnp.int32, (count, count), 0)
    earlier = (before < lane).astype(BF16)
    place_row = lax.broadcasted_iota(jnp.int32, (rows, count), 0).astype(F32)
    caps = [(cap + cap * plan[z * COLS + (x + d) % COLS]).astype(F32) for d in range(COLS)]

    def choose(block, side):
        ids, gates = block[0:8, :], block[8:16, :]
        picks, weights = [], []
        for d in range(COLS):
            expert = (z * COLS + (x + d) % COLS).astype(F32)
            same = ids == expert
            picks.append(jnp.sum(jnp.where(same, 1.0, 0.0), axis=0, keepdims=True))
            weights.append(jnp.sum(jnp.where(same, gates, 0.0), axis=0, keepdims=True))
        picked = jnp.concatenate(picks + [jnp.zeros((8 - COLS, count), F32)], axis=0)
        rank = jnp.dot(picked.astype(BF16), earlier, preferred_element_type=F32)
        chosen = []
        for d in range(COLS):
            kept = (picks[d] > 0.5) & (rank[d : d + 1] < caps[d])
            spot = jnp.where(kept, rank[d : d + 1] + float(side * slots), -1.0)
            chosen.append(
                jnp.where(place_row == spot, jnp.broadcast_to(weights[d], (rows, count)), 0.0)
            )
        return jnp.concatenate(chosen, axis=0)

    row_copies = []
    own_copies = []

    def select(p, a, b):
        spread[p, 0] = choose(a[2], 0)
        spread[p, 1] = choose(b[2], 1)
        scale = jnp.sum(spread[p, 0] + spread[p, 1], axis=1, keepdims=True)
        one_a = jnp.where(spread[p, 0] > 0.0, 1.0, 0.0).astype(BF16)
        one_b = jnp.where(spread[p, 1] > 0.0, 1.0, 0.0).astype(BF16)
        step = 512
        for q, (sel, out) in enumerate(((tok_sel, tok_rows), (cot_sel, cot_rows))):

            @pl.loop(0, width // step)
            def _(i):
                cols = pl.ds(pl.multiple_of(i * step, step), step)
                got = jnp.dot(one_a, a[q][:, cols], preferred_element_type=F32)
                got += jnp.dot(one_b, b[q][:, cols], preferred_element_type=F32)
                if q == 1:
                    got = got * scale
                for d in range(COLS):
                    sel[p, d, :, cols] = got[d * rows : (d + 1) * rows].astype(BF16)

            for d in range(1, COLS):
                copy = copy_to(
                    sel.at[p, d], out.at[d, p], row_send.at[q, p, d - 1],
                    row_recv.at[q, p, d - 1], right[d],
                )
                copy.start()
                row_copies.append(copy)
            mine = pltpu.make_async_copy(sel.at[p, 0], out.at[0, p], own_sem.at[q, p])
            mine.start()
            own_copies.append(mine)

    def block(way, d):
        return tuple(ring[q].at[slot(way, d)] for q in range(3))

    for d in range(1, HOPS + 1):
        for q in (2, 0, 1):
            for way in range(2):
                if (q, way, d) in hops:
                    hops[q, way, d].wait_recv()
                if (q, way, d + 1) in hops:
                    hops[q, way, d + 1].start()
        select(d, block(0, d), block(1, d))
    for q in (2, 0, 1):
        for way in range(2):
            if (q, way, HOPS + 1) in hops:
                hops[q, way, HOPS + 1].wait_recv()
    select(0, own, block(0, HOPS + 1))

    for copy in hops.values():
        copy.wait_send()
    for copy in row_copies:
        copy.wait()
    for copy in own_copies:
        copy.wait()


def dispatch(cap, plan, tok, cot, info):
    count, width = tok.shape
    rows = 4 * cap
    shape = jax.ShapeDtypeStruct((COLS, PAIRS, rows, width), BF16)
    vmem = pl.BlockSpec(memory_space=pltpu.VMEM)
    hbm = pl.BlockSpec(memory_space=pl.ANY)
    return pl.pallas_call(
        functools.partial(dispatch_kernel, cap),
        name="dispatch",
        out_shape=(
            shape,
            shape,
            jax.ShapeDtypeStruct((PAIRS, 2, COLS * rows, count), F32),
        ),
        in_specs=[pl.BlockSpec(memory_space=pltpu.SMEM), vmem, vmem, vmem],
        out_specs=(hbm, hbm, vmem),
        scratch_shapes=[
            pltpu.VMEM((FAR + 1, count, width), BF16),
            pltpu.VMEM((FAR + 1, count, width), BF16),
            pltpu.VMEM((FAR + 1,) + info.shape, F32),
            pltpu.VMEM((PAIRS, COLS, rows, width), BF16),
            pltpu.VMEM((PAIRS, COLS, rows, width), BF16),
            pltpu.SemaphoreType.DMA((3, 2 * (HOPS + 1))),
            pltpu.SemaphoreType.DMA((3, 2 * (HOPS + 1))),
            pltpu.SemaphoreType.DMA((2, PAIRS, COLS - 1)),
            pltpu.SemaphoreType.DMA((2, PAIRS, COLS - 1)),
            pltpu.SemaphoreType.DMA((2, PAIRS)),
        ],
        compiler_params=pltpu.CompilerParams(
            collective_id=0, has_side_effects=True, vmem_limit_bytes=48 * 2**20
        ),
    )(plan, tok, cot, info)


def gather_kernel(
    out_rows, grad_rows, spread, out, grad,
    out_got, grad_got, mix, out_part, grad_part, out_in, grad_in,
    ring_send, ring_recv, row_send, row_recv, own_sem,
):
    z, x, up, down, right, left = place()
    count = spread.shape[3]
    half = count // 2
    meet(up, down, right)

    got = (out_got, grad_got)
    part = (out_part, grad_part)
    into = (out_in, grad_in)
    final = (out, grad)

    row_copies, own_copies = {}, {}
    for p in (0, 3, 2, 1):
        for q, src in enumerate((out_rows, grad_rows)):
            for d in range(1, COLS):
                row_copies[q, p, d] = copy_to(
                    src.at[d, p], got[q].at[p, d], row_send.at[q, p, d - 1],
                    row_recv.at[q, p, d - 1], left[d],
                )
                row_copies[q, p, d].start()
            own_copies[q, p] = pltpu.make_async_copy(
                src.at[0, p], got[q].at[p, 0], own_sem.at[q, p]
            )
            own_copies[q, p].start()

    for p in range(PAIRS):
        for side in range(2):
            turned = jnp.transpose(spread[p, side])
            high = turned.astype(BF16)
            mix[0, p, side] = high
            mix[1, p, side] = (turned - high.astype(F32)).astype(BF16)
            mix[2, p, side] = jnp.where(turned > 0.0, 1.0, 0.0).astype(BF16)

    step = 512

    def columns(q):
        width = got[q].shape[3]
        whole = width // step
        return whole, width - whole * step

    def each(q, body):
        whole, rest = columns(q)

        @pl.loop(0, whole)
        def _(i):
            body(pl.ds(pl.multiple_of(i * step, step), step))

        if rest:
            body(pl.ds(whole * step, rest))

    def combine(q, p, side, cols):
        slots = jnp.concatenate(
            [got[q][p, d, :, cols].astype(F32) for d in range(COLS)], axis=0
        ).astype(BF16)
        if q == 1:
            return jnp.dot(mix[2, p, side], slots, preferred_element_type=F32)
        total = jnp.dot(mix[0, p, side], slots, preferred_element_type=F32)
        return total + jnp.dot(mix[1, p, side], slots, preferred_element_type=F32)

    def hop(q, way, d):
        src, dst = part[q].at[way, d - 1], into[q].at[way, d - 1]
        if d > HOPS:
            src, dst = src.at[pl.ds(way * half, half)], dst.at[pl.ds(way * half, half)]
        sem = way * (HOPS + 1) + d - 1
        return copy_to(
            src, dst, ring_send.at[q, sem], ring_recv.at[q, sem], down if way else up
        )

    hops = {
        (q, way, d): hop(q, way, d)
        for q in range(2)
        for way in range(2)
        for d in range(1, HOPS + 2)
    }

    def arrive(q, p):
        for d in range(1, COLS):
            row_copies[q, p, d].wait_recv()
        own_copies[q, p].wait()

    for q in range(2):
        arrive(q, 0)

        def far(cols, q=q):
            total = combine(q, 0, 1, cols).astype(BF16)
            part[q][0, HOPS, 0:half, cols] = total[:half]
            part[q][1, HOPS, half:, cols] = total[half:]

        each(q, far)
        for way in range(2):
            hops[q, way, HOPS + 1].start()

    for d in range(HOPS, 0, -1):
        for q in range(2):
            arrive(q, d)
            for way in range(2):
                hops[q, way, d + 1].wait_recv()

                def near(cols, q=q, way=way, d=d):
                    total = combine(q, d, 1 - way, cols)
                    if d == HOPS:
                        mine = slice(half, None) if way else slice(0, half)
                        rest = slice(0, half) if way else slice(half, None)
                        there = into[q][way, d, mine, cols].astype(F32)
                        part[q][way, d - 1, mine, cols] = (total[mine] + there).astype(BF16)
                        part[q][way, d - 1, rest, cols] = total[rest].astype(BF16)
                    else:
                        there = into[q][way, d, :, cols].astype(F32)
                        part[q][way, d - 1, :, cols] = (total + there).astype(BF16)

                each(q, near)
                hops[q, way, d].start()

    for q in range(2):
        for way in range(2):
            hops[q, way, 1].wait_recv()

        def last(cols, q=q):
            total = combine(q, 0, 0, cols)
            total = total + into[q][0, 0, :, cols].astype(F32)
            total = total + into[q][1, 0, :, cols].astype(F32)
            final[q][:, cols] = total.astype(BF16)

        each(q, last)

    for copy in hops.values():
        copy.wait_send()
    for copy in row_copies.values():
        copy.wait_send()


def gather(out_rows, grad_rows, spread):
    rows, width = out_rows.shape[2:]
    wide = grad_rows.shape[3]
    count = spread.shape[3]
    vmem = pl.BlockSpec(memory_space=pltpu.VMEM)
    hbm = pl.BlockSpec(memory_space=pl.ANY)
    return pl.pallas_call(
        gather_kernel,
        name="gather",
        out_shape=(
            jax.ShapeDtypeStruct((count, width), BF16),
            jax.ShapeDtypeStruct((count, wide), BF16),
        ),
        in_specs=[hbm, hbm, vmem],
        out_specs=(vmem, vmem),
        scratch_shapes=[
            pltpu.VMEM((PAIRS, COLS, rows, width), BF16),
            pltpu.VMEM((PAIRS, COLS, rows, wide), BF16),
            pltpu.VMEM((3, PAIRS, 2, count, COLS * rows), BF16),
            pltpu.VMEM((2, HOPS + 1, count, width), BF16),
            pltpu.VMEM((2, HOPS + 1, count, wide), BF16),
            pltpu.VMEM((2, HOPS + 1, count, width), BF16),
            pltpu.VMEM((2, HOPS + 1, count, wide), BF16),
            pltpu.SemaphoreType.DMA((2, 2 * (HOPS + 1))),
            pltpu.SemaphoreType.DMA((2, 2 * (HOPS + 1))),
            pltpu.SemaphoreType.DMA((2, PAIRS, COLS - 1)),
            pltpu.SemaphoreType.DMA((2, PAIRS, COLS - 1)),
            pltpu.SemaphoreType.DMA((2, PAIRS)),
        ],
        compiler_params=pltpu.CompilerParams(
            collective_id=1, has_side_effects=True, vmem_limit_bytes=48 * 2**20
        ),
    )(out_rows, grad_rows, spread)


def expert_pass(rows, cots, weights, here):
    gate_part = jnp.dot(rows, weights[0], preferred_element_type=F32)
    up_part = jnp.dot(rows, weights[1], preferred_element_type=F32)
    sigma = jax.nn.sigmoid(gate_part)
    active = gate_part * sigma
    hidden = (active * up_part).astype(BF16)
    contract_last = (((1,), (1,)), ((), ()))
    out = lax.dot_general(hidden, weights[2], contract_last, preferred_element_type=F32)
    hgrad = jnp.dot(cots, weights[2], preferred_element_type=F32)
    d_gate = (hgrad * up_part * sigma * (1.0 + gate_part * (1.0 - sigma))).astype(BF16)
    d_up = (hgrad * active).astype(BF16)
    row_grad = lax.dot_general(d_gate, weights[0], contract_last, preferred_element_type=F32)
    row_grad += lax.dot_general(d_up, weights[1], contract_last, preferred_element_type=F32)
    inner = jnp.sum(hidden.astype(F32) * hgrad, axis=1, keepdims=True)
    lanes = lax.broadcasted_iota(jnp.int32, (rows.shape[0], LANES), 1)
    inner = jnp.where(lanes == here, inner, 0.0)
    grad = jnp.concatenate([row_grad.astype(BF16), inner.astype(BF16)], axis=1)
    contract_rows = (((0,), (0,)), ((), ()))
    upper = lax.dot_general(
        rows, jnp.concatenate([d_gate, d_up], axis=1), contract_rows, preferred_element_type=F32
    )
    lower = lax.dot_general(cots, hidden, contract_rows, preferred_element_type=F32)
    return out.astype(BF16), grad, jnp.concatenate([upper, lower], axis=1).astype(BF16)


def per_device(tokens, expert_ids, gate_vals, replica_plan, expert_weights, cotangent):
    count, width = tokens.shape
    topk = expert_ids.shape[1]
    experts = replica_plan.shape[0]
    hidden_units = expert_weights.shape[3]
    cap = count * topk * 5 // (16 * experts)
    here = lax.axis_index("expert")
    info = jnp.concatenate([expert_ids.astype(F32), gate_vals], axis=1).T
    tok_rows, cot_rows, spread = dispatch(cap, replica_plan, tokens, cotangent, info)
    shape = tok_rows.shape
    out, grad, partial = expert_pass(
        tok_rows.reshape(-1, width), cot_rows.reshape(-1, width), expert_weights[0], here
    )
    per_dev = width // lax.axis_size("dp")
    shard = lax.psum_scatter(partial, "dp", scatter_dimension=0, tiled=True)
    output, wide = gather(
        out.reshape(shape), grad.reshape(shape[:3] + (width + LANES,)), spread
    )
    input_grad = wide[:, :width]
    inner = wide[:, width : width + experts].astype(F32)
    labels = jnp.arange(experts, dtype=jnp.int32)
    same = expert_ids[:, :, None] == labels
    gate_grads = jnp.sum(jnp.where(same, inner[:, None, :], 0.0), axis=2) / gate_vals
    weight_grads = shard.reshape(per_dev, 3, hidden_units).transpose(1, 0, 2)[None]
    return (output, gate_grads, input_grad, weight_grads)


def solution(mesh):
    in_specs = (
        P(("dp", "expert"), None),
        P(("dp", "expert"), None),
        P(("dp", "expert"), None),
        P(),
        P("expert", None, None, None),
        P(("dp", "expert"), None),
    )
    out_specs = (
        P(("dp", "expert"), None),
        P(("dp", "expert"), None),
        P(("dp", "expert"), None),
        P("expert", None, "dp", None),
    )
    return jax.shard_map(
        per_device, mesh=mesh, in_specs=in_specs, out_specs=out_specs, check_vma=False
    )
```

time: 489 us -> 275 us (0.56); the launches traced: 480 us -> 275 us
  waiting for transfers between devices: 251 us -> 0.02 us
  Pallas kernels: 0 us -> 208 us
  local copies, waits for them, and re-layouts: 64.4 us -> 7.22 us
  starting transfers between devices: 53.7 us -> 0.04 us
  other arithmetic: 50.2 us -> 15.4 us
  matrix products: 44.9 us -> 30.1 us
    all_to_all x4 -> x0, waiting for transfers between devices: 251 us -> none  [the longest x1 69 us: per_device(): lax.all_to_all(dy_send.reshape(experts, slots, width), 'expert', split_ax...]
    pallas_call x0 -> x2, Pallas kernels: none -> 208 us  [the longest x1 109 us: dispatch(): pl.pallas_call(functools.partial(dispatch_kernel, cap), name='dispatch',...]
    all_to_all x4 -> x0, starting transfers between devices: 53.7 us -> none  [the longest x1 29.4 us: per_device(): lax.all_to_all(grad_buffer, 'expert', split_axis=0, concat_axis=0, tiled=...]
    reshape x12 -> x1, local copies, waits for them, and re-layouts: 32.7 us -> 2.37 us  [per_device(): shard.reshape(per_dev, 3, hidden_units).transpose(1, 0, 2)[None]]
    reduce_sum x6 -> x1, other arithmetic: 18.7 us -> 0.04 us  [per_device(): jnp.sum(jnp.where(same, inner[:, None, :], 0.0), axis=2) / gate_vals]
    dot_general x10 -> x8, matrix products: 44.9 us -> 30.1 us  [the longest x1 5.4 us: expert_pass(): lax.dot_general(rows, jnp.concatenate([d_gate, d_up], axis=1), contract_r...]
    gather x2 -> x0, local copies, waits for them, and re-layouts: 12 us -> none  [the longest x1 6.02 us: per_device(): jnp.take(grad_back, index, axis=0).astype(jnp.float32)]
    slice x4 -> x1, local copies, waits for them, and re-layouts: 10.3 us -> 0.85 us  [per_device(): input_grad = wide[:, :width]]
  transfers between devices with their start and end apart: 5 -> 1, of which waited for: 4 -> 0; matrix products, arithmetic and copies ran while one was open for 16% -> 6% of each run, Pallas kernels for 0% -> 36%
where the time goes in v1:
time: 275 us
  Pallas kernels  208 us (76%)
  matrix products  30.1 us (11%)
  other arithmetic  15.4 us (6%)
  between operations  14.2 us (5%)
  local copies, waits for them, and re-layouts  7.22 us (3%)
    pallas_call x1, Pallas kernels, dispatch(): pl.pallas_call(functools.partial(dispatch_kernel, cap), name='dispatch',...  109 us
    pallas_call x1, Pallas kernels, gather(): pl.pallas_call(gather_kernel, name='gather', out_shape=(jax.ShapeDtypeStr...  98.4 us
    concatenate x1, other arithmetic, expert_pass(): jnp.concatenate([upper, lower], axis=1).astype(BF16)  11.5 us
  transfers between devices with their start and end apart: 1, of which 0 were waited for; matrix products, arithmetic and copies ran while one was open for 6% of the time, Pallas kernels for 36%

profile of v1, /device:TPU:16, one launch (start us, length us, event | category | flops | bytes accessed | tf_op | source)
XLA Modules:
  0.0 274.7 jit_solution(7829156915678870845)
XLA Ops:
  7.2 0.7 convert_element_type.28
  7.9 0.7 maximum_bitcast_fusion.info
  8.6 1.0 copy-done
  9.6 1.0 copy-done.1
  10.7 0.7 copy-done.2
  11.3 109.3 %dispatch.1 = (bf16[4,4,40,2048]{3,2,1,0:T(8,128)(2,1)S(1)}, bf16[4,4,40,2048]{3,2,1,0:T(8,128)(2,1)}, f32[4,2,160,128]{3,2,1,0:T(8,128)S(1)}) custom-call(s32[32]{0:T(128)S(1)} %copy-done.2, bf16[128,2048]{1,0:T(8,128)(2,1)S(1)} %copy-done, bf16[128,2048]{1,0:T(8,128)(2,1)S(1)} %copy-done.1, f32[16,128]{1,0:T(8,128)S(1)} %maximum_bitcast_fusion.info), custom_call_target="tpu_custom_call" | custom-call | tf_op jit(solution)/shard_map/dispatch/pallas_call | solution.py:178
  120.7 4.2 %fusion.4 = f32[640,768]{1,0:T(8,128)S(1)} fusion(bf16[640,2048]{1,0:T(8,128)(2,1)S(1)} %bitcast.37, bf16[1,3,2048,768]{3,2,1,0:T(8,128)(2,1)} %param.10), kind=kOutput, calls=%fused_computation.9 | convolution fusion | flops 2013265920 | bytes 7733248 | tf_op jit(solution)/shard_map/dot_general | solution.py:378
  124.9 0.4 copy-done.5
  125.3 2.2 fusion.8
  127.5 2.9 %multiply_reduce_fusion = (bf16[640]{0:T(1024)(128)(2,1)S(1)}, bf16[640,768]{1,0:T(8,128)(2,1)S(1)}, bf16[640,768]{1,0:T(8,128)(2,1)S(1)}, bf16[640,768]{1,0:T(8,128)(2,1)S(1)}) fusion(f32[640,768]{1,0:T(8,128)S(1)} %fusion.4, f32[640,768]{1,0:T(8,128)S(1)} %fusion.8, bf16[640,2048]{1,0:T(8,128)(2,1)S(1)} %bitcast.43, ...), kind=kOutput, calls=%fused_computation.25 | convolution fusion | flops 2022112640 | bytes 12649728 | tf_op jit(solution)/shard_map/dot_general | solution.py:384
  130.4 2.9 %convolution_convert_fusion.1 = bf16[2048,768]{0,1:T(8,128)(2,1)S(1)} fusion(bf16[640,2048]{1,0:T(8,128)(2,1)S(1)} %bitcast.44, bf16[640,768]{1,0:T(8,128)(2,1)S(1)} %get-tuple-element.15), kind=kOutput, calls=%fused_computation.3 | convolution fusion | flops 2014838784 | bytes 6750208 | tf_op jit(solution)/shard_map/dot_general | solution.py:397
  133.4 5.4 %convolution_convert_fusion = bf16[2048,1536]{0,1:T(8,128)(2,1)S(1)} fusion(bf16[640,2048]{1,0:T(8,128)(2,1)S(1)} %bitcast.39, bf16[640,768]{1,0:T(8,128)(2,1)S(1)} %get-tuple-element.17, bf16[640,768]{1,0:T(8,128)(2,1)S(1)} %get-tuple-element.16), kind=kOutput, calls=%fused_computation.1 | convolution fusion | flops 4033609728 | bytes 10878976 | tf_op jit(solution)/shard_map/dot_general | solution.py:394
  138.8 11.5 %pad_maximum_fusion = bf16[2048,2304]{0,1:T(8,128)(2,1)} fusion(bf16[2048,768]{0,1:T(8,128)(2,1)S(1)} %convolution_convert_fusion.1, bf16[2048,1536]{0,1:T(8,128)(2,1)S(1)} %convolution_convert_fusion), kind=kLoop, calls=%fused_computation | loop fusion | flops 18874368 | bytes 18874368 | tf_op jit(solution)/shard_map/concatenate | solution.py:398
  150.3 0.1 select_convert_fusion
  150.4 4.2 %fusion.6 = f32[640,2048]{1,0:T(8,128)S(1)} fusion(bf16[640,768]{1,0:T(8,128)(2,1)S(1)} %get-tuple-element.16, bf16[1,3,2048,768]{3,2,1,0:T(8,128)(2,1)} %param.10), kind=kOutput, calls=%fused_computation.11 | convolution fusion | flops 2013265920 | bytes 9371648 | tf_op jit(solution)/shard_map/dot_general | solution.py:387
  154.7 4.1 %add_convert_fusion = bf16[640,2048]{1,0:T(8,128)(2,1)S(1)} fusion(f32[640,2048]{1,0:T(8,128)S(1)} %fusion.6, bf16[640,768]{1,0:T(8,128)(2,1)S(1)} %copy-done.8, bf16[1,3,2048,768]{3,2,1,0:T(8,128)(2,1)} %param.10), kind=kOutput, calls=%fused_computation.2 | convolution fusion | flops 2015887360 | bytes 11993088 | tf_op jit(solution)/shard_map/dot_general | solution.py:388
  158.8 1.8 pad_maximum_fusion.1
  160.6 4.1 %convolution_convert_fusion.2 = bf16[640,2048]{1,0:T(8,128)(2,1)S(1)} fusion(bf16[640,768]{1,0:T(8,128)(2,1)S(1)} %get-tuple-element.15, bf16[1,3,2048,768]{3,2,1,0:T(8,128)(2,1)} %param.10), kind=kOutput, calls=%fused_computation.4 | convolution fusion | flops 2014576640 | bytes 6750208 | tf_op jit(solution)/shard_map/dot_general | solution.py:383
  164.7 98.4 %gather.1 = (bf16[128,2048]{1,0:T(8,128)(2,1)S(1)}, bf16[128,2176]{1,0:T(8,128)(2,1)S(1)}) custom-call(bf16[4,4,40,2048]{3,2,1,0:T(8,128)(2,1)S(1)} %bitcast.36, bf16[4,4,40,2176]{3,2,1,0:T(8,128)(2,1)} %bitcast.40, f32[4,2,160,128]{3,2,1,0:T(8,128)S(1)} %get-tuple-element.11.spread), custom_call_target="tpu_custom_call" | custom-call | tf_op jit(solution)/shard_map/gather/pallas_call | solution.py:347
  263.1 0.8 slice.25
  264.0 0.1 copy.14
  264.1 0.6 div.7
  264.7 2.4 copy.15
  267.0 0.8 copy.17
  (20 shorter events, 0.1 us)
Async XLA Ops:
  7.2 257.5 %reduce-scatter.2.cloned.1.call-start = ((), (), s32[]{:S(2)}) async-start(), calls=%async_computation.1 | async-start | bytes 10616832 | tf_op jit(solution)/shard_map/reduce_scatter | solution.py:415
  8.6 1.0 copy-start
  9.6 1.0 copy-start.1
  10.7 0.7 copy-start.2
  120.7 4.6 %copy-start.5 = (bf16[1,3,2048,768]{3,2,1,0:T(8,128)(2,1)S(1)}, bf16[1,3,2048,768]{3,2,1,0:T(8,128)(2,1)}, u32[]{:S(2)}) copy-start(bf16[1,3,2048,768]{3,2,1,0:T(8,128)(2,1)} %param.10) | copy-start | bytes 28311556
  125.3 2.2 copy-start.6
  130.4 2.9 %copy-start.7 = (bf16[640,768]{1,0:T(8,128)(2,1)}, bf16[640,768]{1,0:T(8,128)(2,1)S(1)}, u32[]{:S(2)}) copy-start(bf16[640,768]{1,0:T(8,128)(2,1)S(1)} %get-tuple-element.17) | copy-start | bytes 2949124
  150.4 4.2 %copy-start.8 = (bf16[640,768]{1,0:T(8,128)(2,1)S(1)}, bf16[640,768]{1,0:T(8,128)(2,1)}, u32[]{:S(2)}) copy-start(bf16[640,768]{1,0:T(8,128)(2,1)} %copy-done.7) | copy-start | bytes 2949124
  164.7 99.3 %copy-start.4 = (s32[128,8]{0,1:T(8,128)S(1)}, s32[128,8]{0,1:T(8,128)}, u32[]{:S(2)}) copy-start(s32[128,8]{0,1:T(8,128)} %param.7) | copy-start | bytes 12292
  164.7 99.4 %copy-start.3 = (f32[128,8]{0,1:T(8,128)S(1)}, f32[128,8]{0,1:T(8,128)}, u32[]{:S(2)}) copy-start(f32[128,8]{0,1:T(8,128)} %param.8) | copy-start | bytes 12292
Sparse Core Ops, SparseCore 0:
  150.4 55.0 reduce-scatter.1
